TPU v7x, 32 devices: a whole 2x2x4 slice. The times are simulated.
32 devices in a mesh: row: 8 (over z, x), col: 4 (over y, core).
Axes of the slice: x: 2, y: 2, z: 4, core: 2. Of those that a mesh axis runs over, the one named last changes fastest.
Arguments:
- tokens: bfloat16 [512, 4096], P('row', 'col'), may hold values from -6 to 6
- gate_weight: bfloat16 [4096, 14336], P('col', 'row'), may hold values from -0.09375 to 0.09375
- up_weight: bfloat16 [4096, 14336], P('col', 'row'), may hold values from -0.09375 to 0.09375
- down_weight: bfloat16 [14336, 4096], P('row', 'col'), may hold values from -0.046875 to 0.046875
- gate_mask: int32 [32, 112], replicated, may hold values 0 or 1
- up_mask: int32 [32, 112], replicated, may hold values 0 or 1
- down_mask: int32 [112, 32], replicated, may hold values 0 or 1
- out_grad: bfloat16 [512, 4096], P('row', 'col'), may hold values from -6 to 6
Outputs:
- mixed: bfloat16 [512, 4096], P('row', 'col')
- input_grad: bfloat16 [512, 4096], P('row', 'col')
- gate_grad: float32 [4096, 14336], P('col', 'row')
- up_grad: float32 [4096, 14336], P('col', 'row')
- down_grad: float32 [14336, 4096], P('row', 'col')
All inputs are finite; a program needn't handle non-finite values.
Results may differ from a plain program's by a relative error of at most 0.0049.
Values may be sent and summed in bfloat16 or wider, within the bound.
No kernel may reach another device: no remote copies, remote signals or barrier semaphores. Data moves between devices by JAX's collectives and lax.ppermute only.
A program may use at most 128 MiB of HBM per device.

v0:
```python
import jax
import jax.numpy as jnp
from jax import lax
from jax.sharding import PartitionSpec as P

BLOCK = 128


def expand_mask(mask, row_start, row_count, col_start, col_count):
    row_block = (row_start + lax.broadcasted_iota(jnp.int32, (row_count, 1), 0)) // BLOCK
    left = (row_block == lax.broadcasted_iota(jnp.int32, (1, mask.shape[0]), 1)).astype(jnp.float32)
    col_block = (col_start + lax.broadcasted_iota(jnp.int32, (1, col_count), 1)) // BLOCK
    right = (lax.broadcasted_iota(jnp.int32, (mask.shape[1], 1), 0) == col_block).astype(
        jnp.float32
    )
    middle = jnp.dot(left, mask.astype(jnp.float32), precision=lax.Precision.HIGHEST)
    return jnp.dot(middle, right, precision=lax.Precision.HIGHEST)


def contract_first(left, right):
    return lax.dot_general(
        left, right, (((0,), (0,)), ((), ())), preferred_element_type=jnp.float32
    )


def contract_last(left, right):
    return lax.dot_general(
        left, right, (((1,), (1,)), ((), ())), preferred_element_type=jnp.float32
    )


def per_device(
    tokens, gate_weight, up_weight, down_weight, gate_mask, up_mask, down_mask, out_grad
):
    row_index = lax.axis_index("row")
    col_index = lax.axis_index("col")
    feat_cols = gate_weight.shape[0]
    unit_cols = gate_weight.shape[1]
    keep_gate = expand_mask(
        gate_mask, col_index * feat_cols, feat_cols, row_index * unit_cols, unit_cols
    )
    keep_up = expand_mask(
        up_mask, col_index * feat_cols, feat_cols, row_index * unit_cols, unit_cols
    )
    keep_down = expand_mask(
        down_mask, row_index * unit_cols, unit_cols, col_index * feat_cols, feat_cols
    )
    zero = jnp.zeros((), jnp.bfloat16)
    kept_both = jnp.concatenate(
        [jnp.where(keep_gate > 0, gate_weight, zero), jnp.where(keep_up > 0, up_weight, zero)],
        axis=1,
    )
    kept_down = jnp.where(keep_down > 0, down_weight, zero)
    gathered = lax.all_gather(tokens, "row", axis=0, tiled=True)
    block = gathered
    both = lax.psum_scatter(
        jnp.dot(block, kept_both, preferred_element_type=jnp.float32),
        "col",
        scatter_dimension=0,
        tiled=True,
    )
    gate = both[:, :unit_cols]
    up_part = both[:, unit_cols:]
    sig = jax.nn.sigmoid(gate)
    hidden = (gate * sig * up_part).astype(jnp.bfloat16)
    hidden_all = lax.all_gather(hidden, "col", axis=0, tiled=True)
    block = hidden_all
    mixed = lax.psum_scatter(
        jnp.dot(block, kept_down, preferred_element_type=jnp.float32),
        "row",
        scatter_dimension=0,
        tiled=True,
    ).astype(jnp.bfloat16)
    grad_all = lax.all_gather(out_grad, "row", axis=0, tiled=True)
    down_grad = keep_down * contract_first(hidden_all, grad_all)
    block = grad_all
    hidden_grad = lax.psum_scatter(
        contract_last(block, kept_down), "col", scatter_dimension=0, tiled=True
    )
    dgate = hidden_grad * up_part * sig * (1.0 + gate * (1.0 - sig))
    dup = hidden_grad * gate * sig
    pre_grad = jnp.concatenate([dgate.astype(jnp.bfloat16), dup.astype(jnp.bfloat16)], axis=1)
    pre_all = lax.all_gather(pre_grad, "col", axis=0, tiled=True)
    weight_both = contract_first(gathered, pre_all)
    gate_grad = keep_gate * weight_both[:, :unit_cols]
    up_grad = keep_up * weight_both[:, unit_cols:]
    block = pre_all
    input_grad = lax.psum_scatter(
        contract_last(block, kept_both), "row", scatter_dimension=0, tiled=True
    ).astype(jnp.bfloat16)
    return (mixed, input_grad, gate_grad, up_grad, down_grad)


def solution(mesh):
    return jax.shard_map(
        per_device,
        mesh=mesh,
        in_specs=(
            P("row", "col"),
            P("col", "row"),
            P("col", "row"),
            P("row", "col"),
            P(),
            P(),
            P(),
            P("row", "col"),
        ),
        out_specs=(
            P("row", "col"),
            P("row", "col"),
            P("col", "row"),
            P("col", "row"),
            P("row", "col"),
        ),
        check_vma=False,
    )
```

profile of v0, /device:TPU:0, one launch (start us, length us, event | category | flops | bytes accessed | tf_op | source)
XLA Modules:
  0.0 412.9 jit_solution(11120879040870394195)
XLA Ops:
  7.2 0.0 all-gather.9.cloned.1.call-start
  7.2 0.7 all-gather.9.cloned.1.call-update
  7.9 0.0 all-gather.5.cloned.1.call-start
  7.9 0.7 all-gather.5.cloned.1.call-update
  8.7 0.0 reduce-scatter.9.cloned.1.call-start
  8.7 1.4 fusion.1
  10.1 5.0 %fusion.11 = f32[1792,1024]{1,0:T(8,128)} fusion(f32[1792,32]{1,0:T(8,128)S(1)} %fusion.1, s32[1024]{0:T(1024)S(1)} %add_select_fusion.1), kind=kOutput, calls=%fused_computation.30 | convolution fusion | flops 704675840 | bytes 7573504 | tf_op jit(solution)/shard_map/dot_general | solution.py:17
  15.2 38.0 %all-gather.9.cloned.1.call-done = bf16[512,1024]{1,0:T(8,128)(2,1)} async-done(((bf16[64,1024]{1,0:T(8,128)(2,1)}), bf16[512,1024]{1,0:T(8,128)(2,1)}) %all-gather.9.cloned.1.call-update) | async-done | bytes 1048592 | tf_op jit(solution)/shard_map/all_gather | solution.py:74
  53.1 8.3 %convolution_bitcast_fusion.2 = f32[512,1792]{0,1:T(8,128)} fusion(bf16[512,1024]{1,0:T(8,128)(2,1)} %all-gather.9.cloned.1.call-done, bf16[1792,1024]{1,0:T(8,128)(2,1)} %param.11, f32[1792,1024]{1,0:T(8,128)} %fusion.11), kind=kOutput, calls=%fused_computation.10 | convolution fusion | flops 1882718208 | bytes 15728640 | tf_op jit(solution)/shard_map/dot_general | solution.py:27
  61.4 0.0 reduce-scatter.9.cloned.1.call-update
  61.4 0.2 reduce-scatter.5.cloned.1.call-start
  61.7 0.5 copy-done.1
  62.1 0.5 fusion.4
  62.6 0.0 copy-done.2
  62.6 0.5 fusion.5
  63.1 0.0 copy-start
  63.1 7.6 %compare_select_fusion.2 = (bf16[1024,1792]{1,0:T(8,128)(2,1)}, f32[1024,1792]{1,0:T(8,128)}) fusion(bf16[1024,1792]{1,0:T(8,128)(2,1)} %param.9, f32[1024,112]{1,0:T(8,128)S(1)} %fusion.5, s32[1792]{0:T(1024)S(1)} %add_select_fusion), kind=kOutput, calls=%fused_computation.6 | convolution fusion | flops 2470121472 | bytes 15145984 | tf_op jit(solution)/shard_map/dot_general | solution.py:17
  70.7 0.0 copy-done
  70.7 5.9 %compare_select_fusion.1 = (bf16[1024,1792]{1,0:T(8,128)(2,1)}, f32[1024,1792]{1,0:T(8,128)}) fusion(bf16[1024,1792]{1,0:T(8,128)(2,1)S(1)} %copy-done, f32[1024,112]{1,0:T(8,128)S(1)} %fusion.4, s32[1792]{0:T(1024)S(1)} %add_select_fusion), kind=kOutput, calls=%fused_computation.5 | convolution fusion | flops 2470121472 | bytes 15145984 | tf_op jit(solution)/shard_map/dot_general | solution.py:17
  76.6 17.7 %all-gather.5.cloned.1.call-done = bf16[512,1024]{1,0:T(8,128)(2,1)} async-done(((bf16[64,1024]{1,0:T(8,128)(2,1)}), bf16[512,1024]{1,0:T(8,128)(2,1)}) %all-gather.5.cloned.1.call-update) | async-done | bytes 1048592 | tf_op jit(solution)/shard_map/all_gather | solution.py:54
  94.3 11.0 %convolution_bitcast_fusion.1 = f32[512,3584]{0,1:T(8,128)} fusion(bf16[512,1024]{1,0:T(8,128)(2,1)} %all-gather.5.cloned.1.call-done, bf16[1024,1792]{1,0:T(8,128)(2,1)} %get-tuple-element.10, bf16[1024,1792]{1,0:T(8,128)(2,1)} %get-tuple-element.12), kind=kOutput, calls=%fused_computation.7 | convolution fusion | flops 3772776448 | bytes 15728640 | tf_op jit(solution)/shard_map/dot_general | solution.py:57
  105.2 0.0 reduce-scatter.5.cloned.1.call-update
  105.3 0.0 all-gather.7.cloned.1.call-start
  105.3 31.3 %reduce-scatter.9.cloned.1.call-done = f32[128,1792]{0,1:T(8,128)} async-done(((f32[512,1792]{0,1:T(8,128)}), f32[128,1792]{0,1:T(8,128)}) %reduce-scatter.9.cloned.1.call-update) | async-done | bytes 917520 | tf_op jit(solution)/shard_map/reduce_scatter | solution.py:77
  136.6 67.0 %reduce-scatter.5.cloned.1.call-done = f32[128,3584]{0,1:T(8,128)} async-done(((f32[512,3584]{0,1:T(8,128)}), f32[128,3584]{0,1:T(8,128)}) %reduce-scatter.5.cloned.1.call-update) | async-done | bytes 1835024 | tf_op jit(solution)/shard_map/reduce_scatter | solution.py:56
  203.7 3.1 multiply_convert_fusion.1
  206.7 0.0 all-gather.7.cloned.1.call-update
  206.8 0.0 all-gather.11.cloned.1.call-start
  206.8 1.0 pad_maximum_fusion.3
  207.8 0.0 all-gather.11.cloned.1.call-update
  207.9 0.0 reduce-scatter.7.cloned.1.call-start
  207.9 20.3 %all-gather.7.cloned.1.call-done = bf16[512,1792]{0,1:T(8,128)(2,1)} async-done(((bf16[128,1792]{0,1:T(8,128)(2,1)}), bf16[512,1792]{0,1:T(8,128)(2,1)}) %all-gather.7.cloned.1.call-update) | async-done | bytes 1835024 | tf_op jit(solution)/shard_map/all_gather | solution.py:66
  228.2 8.2 %fusion.24 = f32[512,1024]{1,0:T(8,128)} fusion(bf16[512,1792]{0,1:T(8,128)(2,1)} %all-gather.7.cloned.1.call-done, bf16[1792,1024]{1,0:T(8,128)(2,1)} %param.11, f32[1792,1024]{1,0:T(8,128)} %fusion.11), kind=kOutput, calls=%fused_computation.55 | convolution fusion | flops 1882718208 | bytes 14942208 | tf_op jit(solution)/shard_map/dot_general | solution.py:69
  236.4 0.0 reduce-scatter.7.cloned.1.call-update
  236.4 0.3 reduce-scatter.11.cloned.1.call-start
  236.7 24.9 %all-gather.11.cloned.1.call-done = bf16[512,3584]{0,1:T(8,128)(2,1)} async-done(((bf16[128,3584]{0,1:T(8,128)(2,1)}), bf16[512,3584]{0,1:T(8,128)(2,1)}) %all-gather.11.cloned.1.call-update) | async-done | bytes 3670032 | tf_op jit(solution)/shard_map/all_gather | solution.py:83
  261.6 9.5 %fusion = f32[512,1024]{1,0:T(8,128)} fusion(bf16[512,3584]{0,1:T(8,128)(2,1)} %all-gather.11.cloned.1.call-done, bf16[1024,1792]{1,0:T(8,128)(2,1)} %get-tuple-element.10, bf16[1024,1792]{1,0:T(8,128)(2,1)} %get-tuple-element.12), kind=kOutput, calls=%fused_computation.8 | convolution fusion | flops 3772776448 | bytes 13107200 | tf_op jit(solution)/shard_map/dot_general | solution.py:27
  271.2 0.0 reduce-scatter.11.cloned.1.call-update
  271.2 0.0 copy-start.3
  271.2 0.0 slice-start.1
  271.2 9.4 %convolution_multiply_fusion = f32[1792,1024]{1,0:T(8,128)} fusion(f32[1792,1024]{1,0:T(8,128)} %fusion.11, bf16[512,1792]{0,1:T(8,128)(2,1)} %all-gather.7.cloned.1.call-done, bf16[512,1024]{1,0:T(8,128)(2,1)} %all-gather.9.cloned.1.call-done), kind=kOutput, calls=%fused_computation.9 | convolution fusion | flops 1880883200 | bytes 17563648 | tf_op jit(solution)/shard_map/dot_general | solution.py:21
  280.6 0.0 copy-done.3
  280.6 7.6 %convolution_bitcast_fusion = f32[1024,3584]{1,0:T(8,128)} fusion(bf16[512,3584]{0,1:T(8,128)(2,1)S(1)} %copy-done.3, bf16[512,1024]{1,0:T(8,128)(2,1)S(1)} %copy-done.4), kind=kOutput, calls=%fused_computation | convolution fusion | flops 3758096384 | bytes 19398656 | tf_op jit(solution)/shard_map/dot_general | solution.py:21
  288.2 14.1 %slice_multiply_fusion = (f32[1024,1792]{1,0:T(8,128)}, f32[1024,1792]{1,0:T(8,128)}) fusion(f32[1024,1792]{1,0:T(8,128)} %get-tuple-element.11, f32[1024,3584]{1,0:T(8,128)} %convolution_bitcast_fusion, f32[1024,1792]{1,0:T(8,128)S(1)} %bitcast.18), kind=kLoop, calls=%fused_computation.1 | loop fusion | flops 3670016 | bytes 44040192 | tf_op jit(solution)/shard_map/mul | solution.py:86
  302.3 31.2 %reduce-scatter.7.cloned.1.call-done = f32[64,1024]{1,0:T(8,128)} async-done(((f32[512,1024]{1,0:T(8,128)}), f32[64,1024]{1,0:T(8,128)}) %reduce-scatter.7.cloned.1.call-update) | async-done | bytes 262160 | tf_op jit(solution)/shard_map/reduce_scatter | solution.py:68
  333.5 1.6 convert_element_type.34
  335.1 69.3 %reduce-scatter.11.cloned.1.call-done = f32[64,1024]{1,0:T(8,128)} async-done(((f32[512,1024]{1,0:T(8,128)}), f32[64,1024]{1,0:T(8,128)}) %reduce-scatter.11.cloned.1.call-update) | async-done | bytes 262160 | tf_op jit(solution)/shard_map/reduce_scatter | solution.py:88
  404.5 1.6 convert_element_type.37
  (10 shorter events, 0.0 us)
Async XLA Ops:
  7.2 46.0 %all-gather.9.cloned.1.call-start = ((), (), s32[]{:S(2)}) async-start(), calls=%async_computation.8 | async-start | bytes 1179648 | tf_op jit(solution)/shard_map/all_gather | solution.py:74
  7.9 86.4 %all-gather.5.cloned.1.call-start = ((), (), s32[]{:S(2)}) async-start(), calls=%async_computation.4 | async-start | bytes 1179648 | tf_op jit(solution)/shard_map/all_gather | solution.py:54
  8.7 128.0 %reduce-scatter.9.cloned.1.call-start = ((), (), s32[]{:S(2)}) async-start(), calls=%async_computation.9 | async-start | bytes 4587520 | tf_op jit(solution)/shard_map/reduce_scatter | solution.py:77
  61.4 0.7 copy-start.1
  61.4 1.2 copy-start.2
  61.4 142.2 %reduce-scatter.5.cloned.1.call-start = ((), (), s32[]{:S(2)}) async-start(), calls=%async_computation.5 | async-start | bytes 9175040 | tf_op jit(solution)/shard_map/reduce_scatter | solution.py:56
  63.1 7.6 %copy-start = (bf16[1024,1792]{1,0:T(8,128)(2,1)S(1)}, bf16[1024,1792]{1,0:T(8,128)(2,1)}, u32[]{:S(2)}) copy-start(bf16[1024,1792]{1,0:T(8,128)(2,1)} %param.10) | copy-start | bytes 11010052
  105.3 123.0 %all-gather.7.cloned.1.call-start = ((), (), s32[]{:S(2)}) async-start(), calls=%async_computation.6 | async-start | bytes 2293760 | tf_op jit(solution)/shard_map/all_gather | solution.py:66
  206.8 54.9 %all-gather.11.cloned.1.call-start = ((), (), s32[]{:S(2)}) async-start(), calls=%async_computation.10 | async-start | bytes 4587520 | tf_op jit(solution)/shard_map/all_gather | solution.py:83
  207.9 125.6 %reduce-scatter.7.cloned.1.call-start = ((), (), s32[]{:S(2)}) async-start(), calls=%async_computation.7 | async-start | bytes 2359296 | tf_op jit(solution)/shard_map/reduce_scatter | solution.py:68
  236.4 168.0 %reduce-scatter.11.cloned.1.call-start = ((), (), s32[]{:S(2)}) async-start(), calls=%async_computation.11 | async-start | bytes 2359296 | tf_op jit(solution)/shard_map/reduce_scatter | solution.py:88
  271.2 17.0 %slice-start = ((s8[7340032]{0:T(1024)(128)(4,1)}), s8[3145728]{0:T(1024)(128)(4,1)S(1)}, s32[]{:S(2)}) async-start(s8[7340032]{0:T(1024)(128)(4,1)} %bitcast.17), calls=%async_computation.12 | async-start | bytes 6291456
  271.2 9.4 %copy-start.3 = (bf16[512,3584]{0,1:T(8,128)(2,1)S(1)}, bf16[512,3584]{0,1:T(8,128)(2,1)}, u32[]{:S(2)}) copy-start(bf16[512,3584]{0,1:T(8,128)(2,1)} %all-gather.11.cloned.1.call-done) | copy-start | bytes 11010052
  271.2 9.4 %copy-start.4 = (bf16[512,1024]{1,0:T(8,128)(2,1)S(1)}, bf16[512,1024]{1,0:T(8,128)(2,1)}, u32[]{:S(2)}) copy-start(bf16[512,1024]{1,0:T(8,128)(2,1)} %all-gather.5.cloned.1.call-done) | copy-start | bytes 3145732
  271.2 17.0 %slice-start.1 = ((s8[7340032]{0:T(1024)(128)(4,1)}), s8[4194304]{0:T(1024)(128)(4,1)S(1)}, s32[]{:S(2)}) async-start(s8[7340032]{0:T(1024)(128)(4,1)} %bitcast.17), calls=%async_computation.13 | async-start | bytes 8388608
Sparse Core Ops, SparseCore 0:
  10.1 42.9 all-gather.8
  55.3 38.9 all-gather.4
  96.8 39.7 reduce-scatter.8
  139.0 64.6 reduce-scatter.4
  206.9 21.3 all-gather.6
  229.6 31.9 all-gather.10
  265.2 68.2 reduce-scatter.6
  337.0 67.3 reduce-scatter.10
where the time goes:
time: 413 us
  waiting for transfers between devices  301 us (73%)
  matrix products  74.7 us (18%)
  other arithmetic  21.4 us (5%)
  between operations  14.2 us (3%)
    reduce_scatter x1, waiting for transfers between devices, per_device(): lax.psum_scatter(contract_last(block, kept_both), 'row', scatter_dimensio...  69.3 us
    reduce_scatter x1, waiting for transfers between devices, per_device(): lax.psum_scatter(jnp.dot(block, kept_both, preferred_element_type=jnp.flo...  67 us
    all_gather x1, waiting for transfers between devices, per_device(): grad_all = lax.all_gather(out_grad, 'row', axis=0, tiled=True)  38 us
    reduce_scatter x1, waiting for transfers between devices, per_device(): lax.psum_scatter(contract_last(block, kept_down), 'col', scatter_dimensio...  31.3 us
    reduce_scatter x1, waiting for transfers between devices, per_device(): lax.psum_scatter(jnp.dot(block, kept_down, preferred_element_type=jnp.flo...  31.2 us
    all_gather x1, waiting for transfers between devices, per_device(): pre_all = lax.all_gather(pre_grad, 'col', axis=0, tiled=True)  24.9 us
    all_gather x1, waiting for transfers between devices, per_device(): hidden_all = lax.all_gather(hidden, 'col', axis=0, tiled=True)  20.3 us
    dot_general x3, matrix products, expand_mask(): return jnp.dot(middle, right, precision=lax.Precision.HIGHEST)  18.6 us
  transfers between devices with their start and end apart: 8, of which 8 were waited for; matrix products, arithmetic and copies ran while one was open for 22% of the time, Pallas kernels for 0%

commit v1 on v0

--- a/solution.py
+++ b/solution.py
@@ -80,7 +80,12 @@
     dgate = hidden_grad * up_part * sig * (1.0 + gate * (1.0 - sig))
     dup = hidden_grad * gate * sig
     pre_grad = jnp.concatenate([dgate.astype(jnp.bfloat16), dup.astype(jnp.bfloat16)], axis=1)
-    pre_all = lax.all_gather(pre_grad, "col", axis=0, tiled=True)
+    ring = [pre_grad]
+    for hop in range(3):
+        ring.append(lax.ppermute(ring[-1], "col", [(dev, (dev + 1) % 4) for dev in range(4)]))
+    pre_all = jnp.roll(
+        jnp.concatenate(ring[::-1], axis=0), (lax.axis_index("col") + 1) * ring[0].shape[0], axis=0
+    )
     weight_both = contract_first(gathered, pre_all)
     gate_grad = keep_gate * weight_both[:, :unit_cols]
     up_grad = keep_up * weight_both[:, unit_cols:]

time: 413 us -> 397 us (0.961)
  waiting for transfers between devices: 301 us -> 282 us
  local copies, waits for them, and re-layouts: 0.49 us -> 7.17 us
    ppermute x0 -> x3, waiting for transfers between devices: none -> 36.9 us  [per_device(): lax.ppermute(ring[-1], 'col', [(dev, (dev + 1) % 4) for dev in range(4)])]
    all_gather x1 -> x0, waiting for transfers between devices: 24.9 us -> none  [per_device(): pre_all = lax.all_gather(pre_grad, 'col', axis=0, tiled=True)]
    all_gather x1, waiting for transfers between devices: 20.3 us -> 0.01 us  [per_device(): hidden_all = lax.all_gather(hidden, 'col', axis=0, tiled=True)]
    reduce_scatter x1, waiting for transfers between devices: 31.2 us -> 20.1 us  [per_device(): lax.psum_scatter(jnp.dot(block, kept_down, preferred_element_type=jnp.flo...]
    unnamed x14 -> x26, local copies, waits for them, and re-layouts: 0.49 us -> 7.17 us
  transfers between devices with their start and end apart: 8 -> 10, of which waited for: 8 -> 9; matrix products, arithmetic and copies ran while one was open for 22% -> 23% of each run, Pallas kernels for 0% -> 0%
where the time goes in v1:
time: 397 us
  waiting for transfers between devices  282 us (71%)
  matrix products  71.2 us (18%)
  other arithmetic  21 us (5%)
  between operations  14.3 us (4%)
  local copies, waits for them, and re-layouts  7.17 us (2%)
    reduce_scatter x1, waiting for transfers between devices, per_device(): lax.psum_scatter(contract_last(block, kept_both), 'row', scatter_dimensio...  69.3 us
    reduce_scatter x1, waiting for transfers between devices, per_device(): lax.psum_scatter(jnp.dot(block, kept_both, preferred_element_type=jnp.flo...  67 us
    all_gather x1, waiting for transfers between devices, per_device(): grad_all = lax.all_gather(out_grad, 'row', axis=0, tiled=True)  38 us
    ppermute x3, waiting for transfers between devices, per_device(): lax.ppermute(ring[-1], 'col', [(dev, (dev + 1) % 4) for dev in range(4)])  36.9 us
    reduce_scatter x1, waiting for transfers between devices, per_device(): lax.psum_scatter(contract_last(block, kept_down), 'col', scatter_dimensio...  31.3 us
    reduce_scatter x1, waiting for transfers between devices, per_device(): lax.psum_scatter(jnp.dot(block, kept_down, preferred_element_type=jnp.flo...  20.1 us
    dot_general x3, matrix products, expand_mask(): return jnp.dot(middle, right, precision=lax.Precision.HIGHEST)  18.6 us
    all_gather x1, waiting for transfers between devices, per_device(): gathered = lax.all_gather(tokens, 'row', axis=0, tiled=True)  18.1 us
  transfers between devices with their start and end apart: 10, of which 9 were waited for; matrix products, arithmetic and copies ran while one was open for 23% of the time, Pallas kernels for 0%

profile of v1, /device:TPU:0, one launch (start us, length us, event | category | flops | bytes accessed | tf_op | source)
XLA Modules:
  0.0 396.7 jit_solution(16815893431431324009)
XLA Ops:
  7.2 0.0 all-gather.8.cloned.1.call-start
  7.2 0.7 all-gather.8.cloned.1.call-update
  7.9 0.0 all-gather.4.cloned.1.call-start
  7.9 0.7 all-gather.4.cloned.1.call-update
  8.7 0.0 reduce-scatter.9.cloned.1.call-start
  8.7 1.4 fusion.3
  10.1 5.0 %fusion.13 = f32[1792,1024]{1,0:T(8,128)} fusion(f32[1792,32]{1,0:T(8,128)S(1)} %fusion.3, s32[1024]{0:T(1024)S(1)} %add_select_fusion.1), kind=kOutput, calls=%fused_computation.32 | convolution fusion | flops 704675840 | bytes 7573504 | tf_op jit(solution)/shard_map/dot_general | solution.py:17
  15.2 38.0 %all-gather.8.cloned.1.call-done = bf16[512,1024]{1,0:T(8,128)(2,1)} async-done(((bf16[64,1024]{1,0:T(8,128)(2,1)}), bf16[512,1024]{1,0:T(8,128)(2,1)}) %all-gather.8.cloned.1.call-update) | async-done | bytes 1048592 | tf_op jit(solution)/shard_map/all_gather | solution.py:74
  53.1 8.3 %convolution_bitcast_fusion.2 = f32[512,1792]{0,1:T(8,128)} fusion(bf16[512,1024]{1,0:T(8,128)(2,1)} %all-gather.8.cloned.1.call-done, bf16[1792,1024]{1,0:T(8,128)(2,1)} %param.11, f32[1792,1024]{1,0:T(8,128)} %fusion.13), kind=kOutput, calls=%fused_computation.10 | convolution fusion | flops 1882718208 | bytes 15728640 | tf_op jit(solution)/shard_map/dot_general | solution.py:27
  61.4 0.0 reduce-scatter.9.cloned.1.call-update
  61.4 0.2 reduce-scatter.5.cloned.1.call-start
  61.7 0.5 fusion.6
  62.2 0.5 fusion.7
  62.6 7.6 %compare_select_fusion.2 = (bf16[1024,1792]{1,0:T(8,128)(2,1)}, f32[1024,1792]{1,0:T(8,128)}) fusion(bf16[1024,1792]{1,0:T(8,128)(2,1)} %param.9, f32[1024,112]{1,0:T(8,128)S(1)} %fusion.7, s32[1792]{0:T(1024)S(1)} %add_select_fusion), kind=kOutput, calls=%fused_computation.6 | convolution fusion | flops 2470121472 | bytes 15145984 | tf_op jit(solution)/shard_map/dot_general | solution.py:17
  70.2 5.9 %compare_select_fusion.1 = (bf16[1024,1792]{1,0:T(8,128)(2,1)}, f32[1024,1792]{1,0:T(8,128)}) fusion(bf16[1024,1792]{1,0:T(8,128)(2,1)S(1)} %copy-done, f32[1024,112]{1,0:T(8,128)S(1)} %fusion.6, s32[1792]{0:T(1024)S(1)} %add_select_fusion), kind=kOutput, calls=%fused_computation.5 | convolution fusion | flops 2470121472 | bytes 15145984 | tf_op jit(solution)/shard_map/dot_general | solution.py:17
  76.2 18.1 %all-gather.4.cloned.1.call-done = bf16[512,1024]{1,0:T(8,128)(2,1)} async-done(((bf16[64,1024]{1,0:T(8,128)(2,1)}), bf16[512,1024]{1,0:T(8,128)(2,1)}) %all-gather.4.cloned.1.call-update) | async-done | bytes 1048592 | tf_op jit(solution)/shard_map/all_gather | solution.py:54
  94.3 11.0 %convolution_bitcast_fusion.1 = f32[512,3584]{0,1:T(8,128)} fusion(bf16[512,1024]{1,0:T(8,128)(2,1)} %all-gather.4.cloned.1.call-done, bf16[1024,1792]{1,0:T(8,128)(2,1)} %get-tuple-element.10, bf16[1024,1792]{1,0:T(8,128)(2,1)} %get-tuple-element.12), kind=kOutput, calls=%fused_computation.7 | convolution fusion | flops 3772776448 | bytes 15728640 | tf_op jit(solution)/shard_map/dot_general | solution.py:57
  105.2 0.0 reduce-scatter.5.cloned.1.call-update
  105.3 0.0 all-gather.6.cloned.1.call-start
  105.3 31.3 %reduce-scatter.9.cloned.1.call-done = f32[128,1792]{0,1:T(8,128)} async-done(((f32[512,1792]{0,1:T(8,128)}), f32[128,1792]{0,1:T(8,128)}) %reduce-scatter.9.cloned.1.call-update) | async-done | bytes 917520 | tf_op jit(solution)/shard_map/reduce_scatter | solution.py:77
  136.6 67.0 %reduce-scatter.5.cloned.1.call-done = f32[128,3584]{0,1:T(8,128)} async-done(((f32[512,3584]{0,1:T(8,128)}), f32[128,3584]{0,1:T(8,128)}) %reduce-scatter.5.cloned.1.call-update) | async-done | bytes 1835024 | tf_op jit(solution)/shard_map/reduce_scatter | solution.py:56
  203.7 3.1 multiply_convert_fusion.1
  206.7 0.0 all-gather.6.cloned.1.call-update
  206.8 0.0 reduce-scatter.7.cloned.1.call-start
  206.8 0.1 pad_maximum_fusion.3
  206.9 0.1 collective-permute-start
  207.0 18.8 %collective-permute-done = bf16[128,3584]{0,1:T(8,128)(2,1)S(1)} collective-permute-done((bf16[128,3584]{0,1:T(8,128)(2,1)S(1)}, bf16[128,3584]{0,1:T(8,128)(2,1)S(1)}, u32[]{:S(2)}, u32[]{:S(2)}) %collective-permute-start) | collective-permute-done | bytes 917536 | tf_op jit(solution)/shard_map/ppermute | solution.py:85
  225.8 13.6 %collective-permute-done.1 = bf16[128,3584]{0,1:T(8,128)(2,1)S(1)} collective-permute-done((bf16[128,3584]{0,1:T(8,128)(2,1)S(1)}, bf16[128,3584]{0,1:T(8,128)(2,1)S(1)}, u32[]{:S(2)}, u32[]{:S(2)}) %collective-permute-start.1) | collective-permute-done | bytes 917536 | tf_op jit(solution)/shard_map/ppermute | solution.py:85
  239.4 8.2 %fusion.28 = f32[512,1024]{1,0:T(8,128)} fusion(bf16[512,1792]{0,1:T(8,128)(2,1)} %all-gather.6.cloned.1.call-done, bf16[1792,1024]{1,0:T(8,128)(2,1)} %param.11, f32[1792,1024]{1,0:T(8,128)} %fusion.13), kind=kOutput, calls=%fused_computation.67 | convolution fusion | flops 1882718208 | bytes 14942208 | tf_op jit(solution)/shard_map/dot_general | solution.py:69
  247.6 0.3 reduce-scatter.11.cloned.1.call-start
  247.9 4.4 %collective-permute-done.2 = bf16[128,3584]{0,1:T(8,128)(2,1)} collective-permute-done((bf16[128,3584]{0,1:T(8,128)(2,1)S(1)}, bf16[128,3584]{0,1:T(8,128)(2,1)}, u32[]{:S(2)}, u32[]{:S(2)}) %collective-permute-start.2) | collective-permute-done | bytes 917536 | tf_op jit(solution)/shard_map/ppermute | solution.py:85
  252.4 1.4 constant_dynamic-update-slice_fusion.7
  253.8 0.3 constant_dynamic-update-slice_fusion.6
  254.1 0.3 constant_dynamic-update-slice_fusion.5
  254.4 0.3 constant_dynamic-update-slice_fusion.4
  254.8 1.5 constant_dynamic-update-slice_fusion.3
  256.3 0.3 constant_dynamic-update-slice_fusion.2
  256.6 0.3 constant_dynamic-update-slice_fusion.1
  256.9 0.3 constant_dynamic-update-slice_fusion
  257.3 2.9 copy-done.3
  260.2 5.4 %fusion = f32[512,1024]{1,0:T(8,128)} fusion(bf16[1024,1792]{1,0:T(8,128)(2,1)S(1)} %copy-done.2, bf16[1024,1792]{1,0:T(8,128)(2,1)S(1)} %copy-done.1, bf16[1024,3584]{0,1:T(8,128)(2,1)S(1)} %constant_dynamic-update-slice_fusion, s32[]{:T(128)S(6)} %select_n.68), kind=kOutput, calls=%fused_computation.8 | convolution fusion | flops 3772776448 | bytes 13107204 | tf_op jit(solution)/shard_map/dot_general | solution.py:27
  265.7 10.0 %convolution_multiply_fusion = f32[1792,1024]{1,0:T(8,128)} fusion(f32[1792,1024]{1,0:T(8,128)} %fusion.13, bf16[512,1792]{0,1:T(8,128)(2,1)} %all-gather.6.cloned.1.call-done, bf16[512,1024]{1,0:T(8,128)(2,1)} %all-gather.8.cloned.1.call-done), kind=kOutput, calls=%fused_computation.9 | convolution fusion | flops 1880883200 | bytes 17563648 | tf_op jit(solution)/shard_map/dot_general | solution.py:21
  275.7 7.5 %convolution_bitcast_fusion = f32[1024,3584]{1,0:T(8,128)} fusion(bf16[512,1024]{1,0:T(8,128)(2,1)S(1)} %copy-done.7, bf16[1024,3584]{0,1:T(8,128)(2,1)S(1)} %copy-done.4, s32[]{:T(128)S(6)} %select_n.68), kind=kOutput, calls=%fused_computation | convolution fusion | flops 3758096384 | bytes 19398660 | tf_op jit(solution)/shard_map/dot_general | solution.py:21
  283.2 14.0 %slice_multiply_fusion = (f32[1024,1792]{1,0:T(8,128)}, f32[1024,1792]{1,0:T(8,128)}) fusion(f32[1024,1792]{1,0:T(8,128)} %get-tuple-element.11, f32[1024,3584]{1,0:T(8,128)} %convolution_bitcast_fusion, f32[1024,1792]{1,0:T(8,128)S(1)} %bitcast.16), kind=kLoop, calls=%fused_computation.1 | loop fusion | flops 3670016 | bytes 44040192 | tf_op jit(solution)/shard_map/mul | solution.py:91
  297.2 20.1 %reduce-scatter.7.cloned.1.call-done = f32[64,1024]{1,0:T(8,128)} async-done(((f32[512,1024]{1,0:T(8,128)}), f32[64,1024]{1,0:T(8,128)}) %reduce-scatter.7.cloned.1.call-update) | async-done | bytes 262160 | tf_op jit(solution)/shard_map/reduce_scatter | solution.py:68
  317.3 1.6 convert_element_type.34
  318.9 69.3 %reduce-scatter.11.cloned.1.call-done = f32[64,1024]{1,0:T(8,128)} async-done(((f32[512,1024]{1,0:T(8,128)}), f32[64,1024]{1,0:T(8,128)}) %reduce-scatter.11.cloned.1.call-update) | async-done | bytes 262160 | tf_op jit(solution)/shard_map/reduce_scatter | solution.py:93
  388.3 1.6 convert_element_type.37
  (27 shorter events, 0.1 us)
Async XLA Ops:
  7.2 46.0 %all-gather.8.cloned.1.call-start = ((), (), s32[]{:S(2)}) async-start(), calls=%async_computation.8 | async-start | bytes 1179648 | tf_op jit(solution)/shard_map/all_gather | solution.py:74
  7.9 86.4 %all-gather.4.cloned.1.call-start = ((), (), s32[]{:S(2)}) async-start(), calls=%async_computation.4 | async-start | bytes 1179648 | tf_op jit(solution)/shard_map/all_gather | solution.py:54
  8.7 128.0 %reduce-scatter.9.cloned.1.call-start = ((), (), s32[]{:S(2)}) async-start(), calls=%async_computation.9 | async-start | bytes 4587520 | tf_op jit(solution)/shard_map/reduce_scatter | solution.py:77
  15.2 46.5 %copy-start.5 = (s32[32,112]{1,0:T(8,128)S(1)}, s32[32,112]{1,0:T(8,128)}, u32[]{:S(2)}) copy-start(s32[32,112]{1,0:T(8,128)} %param.13) | copy-start | bytes 43012
  15.2 47.0 %copy-start.6 = (s32[32,112]{1,0:T(8,128)S(1)}, s32[32,112]{1,0:T(8,128)}, u32[]{:S(2)}) copy-start(s32[32,112]{1,0:T(8,128)} %param.12) | copy-start | bytes 43012
  61.4 142.2 %reduce-scatter.5.cloned.1.call-start = ((), (), s32[]{:S(2)}) async-start(), calls=%async_computation.5 | async-start | bytes 9175040 | tf_op jit(solution)/shard_map/reduce_scatter | solution.py:56
  62.6 7.6 %copy-start = (bf16[1024,1792]{1,0:T(8,128)(2,1)S(1)}, bf16[1024,1792]{1,0:T(8,128)(2,1)}, u32[]{:S(2)}) copy-start(bf16[1024,1792]{1,0:T(8,128)(2,1)} %param.10) | copy-start | bytes 11010052
  105.3 134.2 %all-gather.6.cloned.1.call-start = ((), (), s32[]{:S(2)}) async-start(), calls=%async_computation.6 | async-start | bytes 2293760 | tf_op jit(solution)/shard_map/all_gather | solution.py:66
  206.8 110.5 %reduce-scatter.7.cloned.1.call-start = ((), (), s32[]{:S(2)}) async-start(), calls=%async_computation.7 | async-start | bytes 2359296 | tf_op jit(solution)/shard_map/reduce_scatter | solution.py:68
  206.9 18.9 %collective-permute-start = (bf16[128,3584]{0,1:T(8,128)(2,1)S(1)}, bf16[128,3584]{0,1:T(8,128)(2,1)S(1)}, u32[]{:S(2)}, u32[]{:S(2)}) collective-permute-start(bf16[128,3584]{0,1:T(8,128)(2,1)S(1)} %pad_maximum_fusion.3), channel_id=1, source_target_pairs={{0,1},{1,2},{2,3},{3,0},{4,5},{5,6},{6,7},{7,4},{8,9},{9,10},{10,1... | collective-permute-start | bytes 2752520 | tf_op jit(solution)/shard_map/ppermute | solution.py:85
  225.8 13.6 %collective-permute-start.1 = (bf16[128,3584]{0,1:T(8,128)(2,1)S(1)}, bf16[128,3584]{0,1:T(8,128)(2,1)S(1)}, u32[]{:S(2)}, u32[]{:S(2)}) collective-permute-start(bf16[128,3584]{0,1:T(8,128)(2,1)S(1)} %collective-permute-done), channel_id=1, source_target_pairs={{0,1},{1,2},{2,3},{3,0},{4,5},{5,6},{6,7},{7,4},{8,9},{9,10},{10,1... | collective-permute-start | bytes 2752520 | tf_op jit(solution)/shard_map/ppermute | solution.py:85
  239.4 12.9 %collective-permute-start.2 = (bf16[128,3584]{0,1:T(8,128)(2,1)S(1)}, bf16[128,3584]{0,1:T(8,128)(2,1)}, u32[]{:S(2)}, u32[]{:S(2)}) collective-permute-start(bf16[128,3584]{0,1:T(8,128)(2,1)S(1)} %collective-permute-done.1), channel_id=1, source_target_pairs={{0,1},{1,2},{2,3},{3,0},{4,5},{5,6},{6,7},{7,4},{8,9},{9,10},{10,1... | collective-permute-start | bytes 2752520 | tf_op jit(solution)/shard_map/ppermute | solution.py:85
  247.6 140.6 %reduce-scatter.11.cloned.1.call-start = ((), (), s32[]{:S(2)}) async-start(), calls=%async_computation.10 | async-start | bytes 2359296 | tf_op jit(solution)/shard_map/reduce_scatter | solution.py:93
  247.9 12.3 %copy-start.1 = (bf16[1024,1792]{1,0:T(8,128)(2,1)S(1)}, bf16[1024,1792]{1,0:T(8,128)(2,1)}, u32[]{:S(2)}) copy-start(bf16[1024,1792]{1,0:T(8,128)(2,1)} %get-tuple-element.12) | copy-start | bytes 11010052
  247.9 12.3 %copy-start.2 = (bf16[1024,1792]{1,0:T(8,128)(2,1)S(1)}, bf16[1024,1792]{1,0:T(8,128)(2,1)}, u32[]{:S(2)}) copy-start(bf16[1024,1792]{1,0:T(8,128)(2,1)} %get-tuple-element.10) | copy-start | bytes 11010052
  257.2 2.9 copy-start.3
  265.6 17.6 %slice-start = ((s8[7340032]{0:T(1024)(128)(4,1)}), s8[3145728]{0:T(1024)(128)(4,1)S(1)}, s32[]{:S(2)}) async-start(s8[7340032]{0:T(1024)(128)(4,1)} %bitcast.15), calls=%async_computation.11 | async-start | bytes 6291456
  265.7 10.0 %copy-start.4 = (bf16[1024,3584]{0,1:T(8,128)(2,1)S(1)}, bf16[1024,3584]{0,1:T(8,128)(2,1)}, u32[]{:S(2)}) copy-start(bf16[1024,3584]{0,1:T(8,128)(2,1)} %copy-done.3) | copy-start | bytes 22020100
  265.7 10.0 %copy-start.7 = (bf16[512,1024]{1,0:T(8,128)(2,1)S(1)}, bf16[512,1024]{1,0:T(8,128)(2,1)}, u32[]{:S(2)}) copy-start(bf16[512,1024]{1,0:T(8,128)(2,1)} %all-gather.4.cloned.1.call-done) | copy-start | bytes 3145732
  265.7 17.5 %slice-start.1 = ((s8[7340032]{0:T(1024)(128)(4,1)}), s8[4194304]{0:T(1024)(128)(4,1)S(1)}, s32[]{:S(2)}) async-start(s8[7340032]{0:T(1024)(128)(4,1)} %bitcast.15), calls=%async_computation.12 | async-start | bytes 8388608
Sparse Core Ops, SparseCore 0:
  10.1 42.9 all-gather.7
  55.3 38.9 all-gather.3
  96.8 39.7 reduce-scatter.8
  139.0 64.6 reduce-scatter.4
  206.9 24.7 all-gather.5
  247.7 69.5 reduce-scatter.6
  320.8 67.3 reduce-scatter.10
